TPU v7x, 32 devices: a whole 2x2x4 slice. The times are simulated.
32 devices in a mesh: view: 4 (over z), brick: 8 (over y, x, core).
Axes of the slice: x: 2, y: 2, z: 4, core: 2. Of those that a mesh axis runs over, the one named last changes fastest.
Arguments:
- estimate: float32 [16, 16, 64, 256], P('brick'), may hold values from 0.5 to 2
- views_data: bfloat16 [4, 8, 112, 32, 128], P('view', 'brick'), may hold values from 0.5 to 2
- psf_taps: float32 [4, 3, 31], P('view'), may hold values from 0.02 to 1
- seg_owner: int32 [4, 8, 32, 1], P('view', 'brick'), may hold values from 0 to 7; in each aligned block of 32 rows (0 to 31, 32 to 63, ..., all dimensions but the last counted through in order) at most 8 rows name the same one
- seg_local: int32 [4, 8, 32], P('view', 'brick'), may hold values from 0 to 1
- seg_offset: int32 [4, 8, 32], P('view', 'brick'), may hold values from 0 to 12
- seg_extent: int32 [4, 8, 32], P('view', 'brick'), may hold values from 1 to 4, 112 in all within a row
- view_shift: int32 [4, 2], P('view'), may hold values from 0 to 32
Outputs:
- joined: float32 [16, 16, 64, 256], P('brick')
Inputs may be any that keep to these rules, and one draw needn't show every extreme that they name: `seg_owner`: within one tile's 32 segments no owner is named more than 8 times, and in every draw some tile names one owner exactly 8 times. `seg_extent`: the 32 extents of a tile sum to 112, and some extent is exactly 4.
All inputs are finite; a program needn't handle non-finite values.
Results may differ from a plain program's by a relative error of at most 0.0003.
Values may be sent and summed in bfloat16 or wider, within the bound.
No kernel may reach another device: no remote copies, remote signals or barrier semaphores. Data moves between devices by JAX's collectives and lax.ppermute only.
A program may use at most 128 MiB of HBM per device.

v0:
```python
import jax
import jax.numpy as jnp
from jax import lax
from jax.sharding import PartitionSpec as P

ITERS = 2
EXTMAX = 4


def blur_matrix(tap_values, length):
    centre = tap_values.shape[0] // 2
    positions = jnp.arange(length, dtype=jnp.int32)
    offsets_tab = positions[:, None] - positions[None, :] + centre
    match_table = (
        offsets_tab[:, :, None] == jnp.arange(tap_values.shape[0], dtype=jnp.int32)[None, None, :]
    ).astype(tap_values.dtype)
    return jnp.sum(match_table * tap_values[None, None, :], axis=-1)


def apply_blur(volume, matrices):
    along_z, along_y, along_x = matrices
    highest = lax.Precision.HIGHEST
    volume = jnp.einsum("...xyz,zw->...xyw", volume, along_z, precision=highest)
    volume = jnp.einsum("...xyz,yw->...xwz", volume, along_y, precision=highest)
    volume = jnp.einsum("...xyz,xw->...wyz", volume, along_x, precision=highest)
    return volume


def view_matrices(view_taps, tile_x, tile_y, tile_z):
    normed = view_taps / jnp.sum(view_taps, axis=1, keepdims=True)
    forward = (
        blur_matrix(normed[2], tile_z),
        blur_matrix(normed[1], tile_y),
        blur_matrix(normed[0], tile_x),
    )
    backward = (forward[0].T, forward[1].T, forward[2].T)
    return (forward, backward)


def slot_ranks(owners):
    positions = jnp.arange(owners.shape[-1], dtype=jnp.int32)
    same_owner = owners[..., :, None] == owners[..., None, :]
    earlier = positions[None, :] < positions[:, None]
    return jnp.sum((same_owner & earlier).astype(jnp.int32), axis=-1)


def on_device(
    estimate, views_data, psf_taps, seg_owner, seg_local, seg_offset, seg_extent, view_shift
):
    per_owner, brick_x, brick_y, brick_z = estimate.shape
    tile_x, tile_y, tile_z = (views_data.shape[2], views_data.shape[3], views_data.shape[4])
    seg_count = seg_extent.shape[2]
    brick_count = lax.axis_size("brick")
    owner_me = lax.axis_index("brick")
    capacity = max(2, 2 * seg_count // brick_count)
    slot_rows = capacity * EXTMAX
    own_rows = per_owner * brick_x
    forward, backward = view_matrices(psf_taps[0], tile_x, tile_y, tile_z)
    shift_y = view_shift[0, 0]
    shift_z = view_shift[0, 1]
    measured = views_data[0, 0].astype(jnp.float32)
    lists = (
        lax.all_gather(seg_owner[:, :, :, 0], "brick", axis=1, tiled=True),
        lax.all_gather(seg_local, "brick", axis=1, tiled=True),
        lax.all_gather(seg_offset, "brick", axis=1, tiled=True),
        lax.all_gather(seg_extent, "brick", axis=1, tiled=True),
    )
    all_owner, all_local, all_offset, all_extent = (
        lists[0][0],
        lists[1][0],
        lists[2][0],
        lists[3][0],
    )
    own_owner = seg_owner[0, 0, :, 0]
    own_local = seg_local[0, 0]
    own_offset = seg_offset[0, 0]
    own_extent = seg_extent[0, 0]
    own_rank = slot_ranks(own_owner)
    seg_ids = jnp.arange(seg_count, dtype=jnp.int32)
    peer_ids = jnp.arange(brick_count, dtype=jnp.int32)
    slot_ids = jnp.arange(capacity, dtype=jnp.int32)
    row_steps = jnp.arange(EXTMAX, dtype=jnp.int32)
    starts = jnp.cumsum(own_extent) - own_extent
    tile_rows = jnp.arange(tile_x, dtype=jnp.int32)
    seg_of = jnp.sum((starts[None, :] <= tile_rows[:, None]).astype(jnp.int32), axis=1) - 1
    within = tile_rows - starts[seg_of]
    source_of_row = (
        (own_owner[seg_of] * per_owner + own_local[seg_of]) * brick_x + own_offset[seg_of] + within
    )
    back_match = (own_owner[None, None, :] == peer_ids[:, None, None]) & (
        own_rank[None, None, :] == slot_ids[None, :, None]
    )
    back_valid = jnp.any(back_match, axis=-1)
    back_seg = jnp.sum(back_match.astype(jnp.int32) * seg_ids, axis=-1)
    back_mask = back_valid[:, :, None] & (
        row_steps[None, None, :] < own_extent[back_seg][:, :, None]
    )
    back_rows = jnp.where(
        back_mask, starts[back_seg][:, :, None] + row_steps[None, None, :], 0
    ).reshape(-1)
    back_mask = back_mask.reshape(-1)
    all_rank = slot_ranks(all_owner)
    owner_match = (all_owner[:, None, :] == owner_me) & (
        all_rank[:, None, :] == slot_ids[None, :, None]
    )
    owner_valid = jnp.any(owner_match, axis=-1)
    owner_seg = jnp.sum(owner_match.astype(jnp.int32) * seg_ids, axis=-1)
    owner_base = jnp.take_along_axis(all_local, owner_seg, axis=1) * brick_x + jnp.take_along_axis(
        all_offset, owner_seg, axis=1
    )
    owner_ext = jnp.take_along_axis(all_extent, owner_seg, axis=1)
    owner_mask = owner_valid[:, :, None] & (row_steps[None, None, :] < owner_ext[:, :, None])
    owner_rows = jnp.where(
        owner_mask, owner_base[:, :, None] + row_steps[None, None, :], 0
    ).reshape(-1)
    owner_mask = owner_mask.reshape(-1)
    landing = (
        (owner_rows[None, :] == jnp.arange(own_rows, dtype=jnp.int32)[:, None])
        & owner_mask[None, :]
    ).astype(jnp.float32)

    def to_owners(projected):
        outgoing = jnp.where(back_mask[:, None, None], jnp.take(projected, back_rows, axis=0), 0.0)
        outgoing = outgoing.reshape(brick_count, slot_rows, tile_y, tile_z)
        arrived = lax.all_to_all(
            outgoing, "brick", split_axis=0, concat_axis=0, tiled=True
        ).reshape(-1, tile_y, tile_z)
        accumulated = jnp.einsum("pq,qyz->pyz", landing, arrived, precision=lax.Precision.HIGHEST)
        brick_part = lax.dynamic_update_slice(
            jnp.zeros((own_rows, brick_y, brick_z), jnp.float32), accumulated, (0, shift_y, shift_z)
        )
        brick_part = brick_part.reshape(per_owner, brick_x, brick_y, brick_z)
        return lax.psum(brick_part, "view")

    weight = to_owners(apply_blur(jnp.ones((tile_x, tile_y, tile_z), jnp.float32), backward))
    current = estimate
    for sweep in range(ITERS):
        flat_est = current.reshape(own_rows, brick_y, brick_z)
        cropped = lax.dynamic_slice(
            flat_est, (0, shift_y, shift_z), (own_rows, tile_y, tile_z)
        ).astype(jnp.bfloat16)
        gathered = lax.all_gather(cropped, "brick", axis=0, tiled=True)
        view_tile = jnp.take(gathered, source_of_row, axis=0)
        correction_view_tile = view_tile.astype(jnp.float32)
        quotient = measured / apply_blur(correction_view_tile, forward)
        correction = to_owners(apply_blur(quotient, backward))
        current = current * (1.0 + correction) / (1.0 + weight)
    return current


def solution(mesh):
    placed = (
        P("brick", None, None, None),
        P("view", "brick", None, None, None),
        P("view", None, None),
        P("view", "brick", None, None),
        P("view", "brick", None),
        P("view", "brick", None),
        P("view", "brick", None),
        P("view", None),
    )
    return jax.shard_map(
        on_device,
        mesh=mesh,
        in_specs=placed,
        out_specs=P("brick", None, None, None),
        check_vma=False,
    )
```

profile of v0, /device:TPU:0, one launch (start us, length us, event | category | flops | bytes accessed | tf_op | source)
XLA Modules:
  0.0 637.1 jit_solution(17363092485871562912)
XLA Ops:
  31.5 3.0 gather_fusion.11
  34.6 10.2 %all-gather.4.cloned.1.call-done = bf16[256,32,128]{2,1,0:T(8,128)(2,1)} async-done(((bf16[32,32,128]{2,1,0:T(8,128)(2,1)}), bf16[256,32,128]{2,1,0:T(8,128)(2,1)}) %all-gather.4.cloned.1.call-update) | async-done | bytes 2097168 | tf_op jit(solution)/shard_map/all_gather | solution.py:142
  49.8 3.1 convert_divide_fusion.1
  59.9 3.0 gather_fusion.10
  62.8 16.0 %select_select_fusion.1 = (f32[256,32,128]{2,1,0:T(8,128)S(1)}, f32[256,32,128]{2,1,0:T(8,128)}) fusion(f32[256,32,128]{2,1,0:T(8,128)} %gather_fusion.11, pred[256]{0:T(512)(128)(4,1)S(1)} %get-tuple-element.12, pred[256]{0:T(512)(128)(4,1)S(1)} %and.102, f32[256,32,128]{2,1,0:T(8,128)} %gather_fusion.10), kind=kLoop, calls=%fused_computation.15 | loop fusion | flops 4194304 | bytes 16777728 | tf_op jit(solution)/shard_map/jit(_where)/select_n | solution.py:123
  78.8 4.3 copy.69
  83.2 4.5 all-to-all-start.1
  87.7 6.5 %copy.64 = f32[8,32,32,128]{3,1,2,0:T(8,128)} copy(f32[8,32,32,128]{3,2,1,0:T(8,128)} %bitcast.133) | data formatting | bytes 8388608 | tf_op jit(solution)/shard_map/reshape | solution.py:124
  94.3 42.6 %all-to-all-done.1 = f32[8,32,32,128]{3,1,2,0:T(8,128)} async-done(((f32[8,32,32,128]{3,1,2,0:T(8,128)}), f32[8,32,32,128]{3,1,2,0:T(8,128)}, u32[]{:S(2)}, u32[]{:S(2)}) %all-to-all-start.1) | async-done | bytes 4194336 | tf_op jit(solution)/shard_map/all_to_all | solution.py:125
  136.8 4.6 all-to-all-start
  141.5 52.0 %all-gather = s32[1,8,32,1]{2,3,0,1:T(1,128)S(1)} all-gather(s32[1,1,32,1]{2,3,0,1:T(1,128)S(1)} %bitcast.124), channel_id=2, replica_groups=mesh['view'=4,'brick'=8] {'brick'}, dimensions={1}, use_global_device_ids=true | all-gather | bytes 1152 | tf_op jit(solution)/shard_map/all_gather | solution.py:63
  194.1 7.9 %all_gather.20 = s32[1,8,32]{2,0,1:T(1,128)S(1)} all-gather(s32[1,1,32]{2,0,1:T(1,128)S(1)} %bitcast.126), channel_id=1, replica_groups=mesh['view'=4,'brick'=8] {'brick'}, dimensions={1}, use_global_device_ids=true | all-gather | bytes 1152 | tf_op jit(solution)/shard_map/all_gather | solution.py:64
  202.8 8.7 %all_gather.21 = s32[1,8,32]{2,0,1:T(1,128)S(1)} all-gather(s32[1,1,32]{2,0,1:T(1,128)S(1)} %bitcast.128), channel_id=1, replica_groups=mesh['view'=4,'brick'=8] {'brick'}, dimensions={1}, use_global_device_ids=true | all-gather | bytes 1152 | tf_op jit(solution)/shard_map/all_gather | solution.py:65
  212.3 7.9 %all_gather.19 = s32[1,8,32]{2,0,1:T(1,128)S(1)} all-gather(s32[1,1,32]{2,0,1:T(1,128)S(1)} %bitcast.117), channel_id=1, replica_groups=mesh['view'=4,'brick'=8] {'brick'}, dimensions={1}, use_global_device_ids=true | all-gather | bytes 1152 | tf_op jit(solution)/shard_map/all_gather | solution.py:66
  231.5 13.4 %dynamic_update_slice.10 = f32[32,64,256]{2,1,0:T(8,128)S(1)} dynamic-update-slice(f32[32,64,256]{2,1,0:T(8,128)S(1)} %broadcast.183.clone.1, f32[32,32,128]{2,1,0:T(8,128)S(1)} %copy.71, s32[]{:T(128)} %constant.39.clone.1, s32[]{:T(128)S(6)} %select_n.82, s32[]{:T(128)S(6)} %select_n.83) | dynamic-update-slice | bytes 1048580 | tf_op jit(solution)/shard_map/dynamic_update_slice | solution.py:129
  246.6 13.9 %dynamic_update_slice.9 = f32[32,64,256]{2,1,0:T(8,128)} dynamic-update-slice(f32[32,64,256]{2,1,0:T(8,128)} %broadcast.183.clone, f32[32,32,128]{2,1,0:T(8,128)S(1)} %copy.66, s32[]{:T(128)} %constant.39.clone.1, s32[]{:T(128)S(6)} %select_n.82, s32[]{:T(128)S(6)} %select_n.83) | dynamic-update-slice | bytes 1048580 | tf_op jit(solution)/shard_map/dynamic_update_slice | solution.py:129
  260.6 154.2 %all-reduce.6.cloned.1.call-done = (f32[2,16,64,256]{3,2,1,0:T(8,128)}, f32[2,16,64,256]{3,2,1,0:T(8,128)}) async-done(((f32[2,16,64,256]{3,2,1,0:T(8,128)}, f32[2,16,64,256]{3,2,1,0:T(8,128)}), (f32[2,16,64,256]{3,2,1,0:T(8,128)}, f32[2,16,64,256]{3,2,1,0:T(8,128)})) %all-reduce.6.cloned.1.call-update) | async-done | bytes 4194320 | tf_op jit(solution)/shard_map/psum | solution.py:133
  414.8 3.5 multiply_divide_fusion.1
  420.7 26.6 %all-gather.6.cloned.1.call-done = bf16[256,32,128]{2,1,0:T(8,128)(2,1)} async-done(((bf16[32,32,128]{2,1,0:T(8,128)(2,1)}), bf16[256,32,128]{2,1,0:T(8,128)(2,1)}) %all-gather.6.cloned.1.call-update) | async-done | bytes 2097168 | tf_op jit(solution)/shard_map/all_gather | solution.py:142
  465.5 3.8 select_select_fusion
  471.6 51.6 %all_to_all.15 = f32[8,32,32,128]{3,1,2,0:T(8,128)S(1)} all-to-all(f32[8,32,32,128]{3,1,2,0:T(8,128)S(1)} %copy.78), channel_id=1, replica_groups=mesh['view'=4,'brick'=8] {'brick'}, dimensions={0} | all-to-all | bytes 8388608 | tf_op jit(solution)/shard_map/all_to_all | solution.py:125
  527.3 14.1 %dynamic_update_slice.11 = f32[32,64,256]{2,1,0:T(8,128)} dynamic-update-slice(f32[32,64,256]{2,1,0:T(8,128)} %broadcast.183, f32[32,32,128]{2,1,0:T(8,128)S(1)} %copy.80, s32[]{:T(128)} %constant.39.clone.1, s32[]{:T(128)S(6)} %select_n.82, s32[]{:T(128)S(6)} %select_n.83) | dynamic-update-slice | bytes 1048580 | tf_op jit(solution)/shard_map/dynamic_update_slice | solution.py:129
  541.4 84.5 %all-reduce.4.cloned.1.call-done = f32[2,16,64,256]{3,2,1,0:T(8,128)} async-done(((f32[2,16,64,256]{3,2,1,0:T(8,128)}), f32[2,16,64,256]{3,2,1,0:T(8,128)}) %all-reduce.4.cloned.1.call-update) | async-done | bytes 2097168 | tf_op jit(solution)/shard_map/psum | solution.py:133
  625.9 4.2 multiply_divide_fusion
  (125 shorter events, 75.0 us)
Async XLA Ops:
  6.5 12.1 %copy-start.1 = (s32[1,1,32,1]{2,3,1,0:T(1,128)S(1)}, s32[1,1,32,1]{2,3,1,0:T(1,128)}, u32[]{:S(2)}) copy-start(s32[1,1,32,1]{2,3,1,0:T(1,128)} %param.17) | copy-start | bytes 388
  6.5 12.3 %copy-start.2 = (s32[1,1,32]{2,1,0:T(1,128)S(1)}, s32[1,1,32]{2,1,0:T(1,128)}, u32[]{:S(2)}) copy-start(s32[1,1,32]{2,1,0:T(1,128)} %param.18) | copy-start | bytes 388
  6.5 13.5 %copy-start.3 = (s32[1,1,32]{2,1,0:T(1,128)S(1)}, s32[1,1,32]{2,1,0:T(1,128)}, u32[]{:S(2)}) copy-start(s32[1,1,32]{2,1,0:T(1,128)} %param.19) | copy-start | bytes 388
  6.5 38.2 %all-gather.4.cloned.1.call-start = ((), (), s32[]{:S(2)}) async-start(), calls=%async_computation.3 | async-start | bytes 2359296 | tf_op jit(solution)/shard_map/all_gather | solution.py:142
  21.6 0.8 copy-start
  22.4 1.6 copy-start.7
  48.1 1.7 copy-start.8
  83.2 53.6 %all-to-all-start.1 = ((f32[8,32,32,128]{3,1,2,0:T(8,128)}), f32[8,32,32,128]{3,1,2,0:T(8,128)}, u32[]{:S(2)}, u32[]{:S(2)}) async-start(f32[8,32,32,128]{3,1,2,0:T(8,128)} %copy.69), calls=%async_computation.1 | async-start | bytes 8388608 | tf_op jit(solution)/shard_map/all_to_all | solution.py:125
  136.8 89.6 %all-to-all-start = ((f32[8,32,32,128]{3,1,2,0:T(8,128)}), f32[8,32,32,128]{3,1,2,0:T(8,128)}, u32[]{:S(2)}, u32[]{:S(2)}) async-start(f32[8,32,32,128]{3,1,2,0:T(8,128)} %copy.64), calls=%async_computation | async-start | bytes 8388608 | tf_op jit(solution)/shard_map/all_to_all | solution.py:125
  141.4 273.3 %all-reduce.6.cloned.1.call-start = ((), (), s32[]{:S(2)}) async-start(), calls=%async_computation.6 | async-start | bytes 8388608 | tf_op jit(solution)/shard_map/psum | solution.py:133
  244.9 15.6 %copy-start.6 = (f32[32,64,256]{2,1,0:T(8,128)}, f32[32,64,256]{2,1,0:T(8,128)S(1)}, u32[]{:S(2)}) copy-start(f32[32,64,256]{2,1,0:T(8,128)S(1)} %dynamic_update_slice.10) | copy-start | bytes 6291460
  260.5 186.9 %all-gather.6.cloned.1.call-start = ((), (), s32[]{:S(2)}) async-start(), calls=%async_computation.4 | async-start | bytes 2359296 | tf_op jit(solution)/shard_map/all_gather | solution.py:142
  418.2 1.3 copy-start.4
  420.5 205.4 %all-reduce.4.cloned.1.call-start = ((), (), s32[]{:S(2)}) async-start(), calls=%async_computation.5 | async-start | bytes 4194304 | tf_op jit(solution)/shard_map/psum | solution.py:133
  450.7 1.7 copy-start.9
  527.3 98.5 %copy-start.5 = (f32[2,16,64,256]{3,2,1,0:T(8,128)S(1)}, f32[2,16,64,256]{3,2,1,0:T(8,128)}, u32[]{:S(2)}) copy-start(f32[2,16,64,256]{3,2,1,0:T(8,128)} %copy-done.4) | copy-start | bytes 6291460
Sparse Core Ops, SparseCore 0:
  14.2 30.5 all-gather.3
  260.6 154.0 all-reduce.5
  420.6 26.7 all-gather.5
  541.5 84.2 all-reduce.3
where the time goes:
time: 648 us; the launch traced here: 637 us
  waiting for transfers between devices  318 us (49%)
  blocking collectives  128 us (20%)
  local copies, waits for them, and re-layouts  97.2 us (15%)
  matrix products  35 us (5%)
  other arithmetic  31.1 us (5%)
  between operations  18.1 us (3%)
  starting transfers between devices  9.48 us (1%)
    psum x2, waiting for transfers between devices, to_owners(): return lax.psum(brick_part, 'view')  239 us
    all_gather x1, blocking collectives, on_device(): lax.all_gather(seg_owner[:, :, :, 0], 'brick', axis=1, tiled=True)  52 us
    all_to_all x1, blocking collectives, to_owners(): lax.all_to_all(outgoing, 'brick', split_axis=0, concat_axis=0, tiled=True)  51.6 us
    all_to_all x2, waiting for transfers between devices, to_owners(): lax.all_to_all(outgoing, 'brick', split_axis=0, concat_axis=0, tiled=True)  42.6 us
    dynamic_update_slice x3, local copies, waits for them, and re-layouts, to_owners(): lax.dynamic_update_slice(jnp.zeros((own_rows, brick_y, brick_z), jnp.floa...  41.3 us
    all_gather x2, waiting for transfers between devices, on_device(): gathered = lax.all_gather(cropped, 'brick', axis=0, tiled=True)  36.9 us
    select_n x2, other arithmetic, to_owners(): jnp.where(back_mask[:, None, None], jnp.take(projected, back_rows, axis=0...  19.7 us
    dot_general x5, matrix products, apply_blur(): volume = jnp.einsum('...xyz,xw->...wyz', volume, along_x, precision=highest)  14.2 us
  transfers between devices with their start and end apart: 6, of which 5 were waited for; matrix products, arithmetic and copies ran while one was open for 6% of the time, Pallas kernels for 0%

commit v1 on v0

--- a/solution.py
+++ b/solution.py
@@ -5,6 +5,27 @@
 
 ITERS = 2
 EXTMAX = 4
+
+
+def _move_ports(sheet, join_dim):
+    z = list(sheet.shape[1:])
+    z[join_dim] *= sheet.shape[0]
+    outer = jnp.moveaxis(sheet, 0, join_dim).reshape(z)
+    return outer
+
+
+def lift_the_tracks(my_tile, axis_id, out_dim=0):
+    n_slots = lax.axis_size(axis_id)
+    ledger = [(num, (num + 1) % n_slots) for num in range(n_slots)]
+    entries = [my_tile]
+    while len(entries) < n_slots:
+        y2 = lax.ppermute(entries[-1], perm=ledger, axis_name=axis_id)
+        entries.append(y2)
+    u1 = lax.axis_index(axis_id)
+    r_now = jnp.stack(entries, axis=0)
+    entries = r_now[(u1 - jnp.arange(n_slots)) % n_slots]
+    field_out = _move_ports(entries, out_dim)
+    return field_out
 
 
 def blur_matrix(tap_values, length):
@@ -139,7 +160,7 @@
         cropped = lax.dynamic_slice(
             flat_est, (0, shift_y, shift_z), (own_rows, tile_y, tile_z)
         ).astype(jnp.bfloat16)
-        gathered = lax.all_gather(cropped, "brick", axis=0, tiled=True)
+        gathered = lift_the_tracks(cropped, "brick")
         view_tile = jnp.take(gathered, source_of_row, axis=0)
         correction_view_tile = view_tile.astype(jnp.float32)
         quotient = measured / apply_blur(correction_view_tile, forward)

time: 648 us -> 685 us (1.057)
  waiting for transfers between devices: 318 us -> 347 us
  local copies, waits for them, and re-layouts: 97.2 us -> 111 us
  other arithmetic: 31.1 us -> 22.3 us
    ppermute x0 -> x14, waiting for transfers between devices: none -> 65.6 us  [lift_the_tracks(): y2 = lax.ppermute(entries[-1], perm=ledger, axis_name=axis_id)]
    all_gather x2 -> x0, waiting for transfers between devices: 36.9 us -> none  [on_device(): gathered = lax.all_gather(cropped, 'brick', axis=0, tiled=True)]
    unnamed x20 -> x36, local copies, waits for them, and re-layouts: 1.35 us -> 13.1 us
    select_n x2, other arithmetic: 19.7 us -> 9.59 us  [to_owners(): jnp.where(back_mask[:, None, None], jnp.take(projected, back_rows, axis=0...]
  transfers between devices with their start and end apart: 6 -> 18, of which waited for: 5 -> 16; matrix products, arithmetic and copies ran while one was open for 6% -> 7% of each run, Pallas kernels for 0% -> 0%
where the time goes in v1:
time: 685 us; the launch traced here: 676 us
  waiting for transfers between devices  347 us (51%)
  blocking collectives  128 us (19%)
  local copies, waits for them, and re-layouts  111 us (16%)
  matrix products  36.3 us (5%)
  other arithmetic  22.3 us (3%)
  between operations  18.3 us (3%)
  starting transfers between devices  12.8 us (2%)
    psum x2, waiting for transfers between devices, to_owners(): return lax.psum(brick_part, 'view')  239 us
    ppermute x14, waiting for transfers between devices, lift_the_tracks(): y2 = lax.ppermute(entries[-1], perm=ledger, axis_name=axis_id)  65.6 us
    all_gather x1, blocking collectives, on_device(): lax.all_gather(seg_owner[:, :, :, 0], 'brick', axis=1, tiled=True)  52 us
    all_to_all x1, blocking collectives, to_owners(): lax.all_to_all(outgoing, 'brick', split_axis=0, concat_axis=0, tiled=True)  51.6 us
    all_to_all x2, waiting for transfers between devices, to_owners(): lax.all_to_all(outgoing, 'brick', split_axis=0, concat_axis=0, tiled=True)  42.6 us
    dynamic_update_slice x3, local copies, waits for them, and re-layouts, to_owners(): lax.dynamic_update_slice(jnp.zeros((own_rows, brick_y, brick_z), jnp.floa...  41.4 us
    dot_general x5, matrix products, apply_blur(): volume = jnp.einsum('...xyz,xw->...wyz', volume, along_x, precision=highest)  15.6 us
  transfers between devices with their start and end apart: 18, of which 16 were waited for; matrix products, arithmetic and copies ran while one was open for 7% of the time, Pallas kernels for 0%

profile of v1, /device:TPU:0, one launch (start us, length us, event | category | flops | bytes accessed | tf_op | source)
XLA Modules:
  0.0 675.6 jit_solution(17289332795131788567)
XLA Ops:
  50.1 5.3 collective-permute-done.4
  56.8 5.3 collective-permute-done.5
  63.7 5.2 collective-permute-done.6
  88.7 5.8 select_select_fusion.1
  103.4 6.5 copy.64
  109.9 42.6 %all-to-all-done.1 = f32[8,32,32,128]{3,1,2,0:T(8,128)} async-done(((f32[8,32,32,128]{3,1,2,0:T(8,128)}), f32[8,32,32,128]{3,1,2,0:T(8,128)}, u32[]{:S(2)}, u32[]{:S(2)}) %all-to-all-start.1) | async-done | bytes 4194336 | tf_op jit(solution)/shard_map/all_to_all | solution.py:146
  152.5 4.6 all-to-all-start
  157.2 52.0 %all-gather = s32[1,8,32,1]{2,3,0,1:T(1,128)S(1)} all-gather(s32[1,1,32,1]{2,3,0,1:T(1,128)S(1)} %bitcast.160), channel_id=2, replica_groups=mesh['view'=4,'brick'=8] {'brick'}, dimensions={1}, use_global_device_ids=true | all-gather | bytes 1152 | tf_op jit(solution)/shard_map/all_gather | solution.py:84
  209.8 7.9 %all_gather.14 = s32[1,8,32]{2,0,1:T(1,128)S(1)} all-gather(s32[1,1,32]{2,0,1:T(1,128)S(1)} %bitcast.162), channel_id=1, replica_groups=mesh['view'=4,'brick'=8] {'brick'}, dimensions={1}, use_global_device_ids=true | all-gather | bytes 1152 | tf_op jit(solution)/shard_map/all_gather | solution.py:85
  218.5 8.7 %all_gather.15 = s32[1,8,32]{2,0,1:T(1,128)S(1)} all-gather(s32[1,1,32]{2,0,1:T(1,128)S(1)} %bitcast.164), channel_id=1, replica_groups=mesh['view'=4,'brick'=8] {'brick'}, dimensions={1}, use_global_device_ids=true | all-gather | bytes 1152 | tf_op jit(solution)/shard_map/all_gather | solution.py:86
  228.0 8.1 %all_gather.13 = s32[1,8,32]{2,0,1:T(1,128)S(1)} all-gather(s32[1,1,32]{2,0,1:T(1,128)S(1)} %bitcast.153), channel_id=1, replica_groups=mesh['view'=4,'brick'=8] {'brick'}, dimensions={1}, use_global_device_ids=true | all-gather | bytes 1152 | tf_op jit(solution)/shard_map/all_gather | solution.py:87
  248.1 13.4 %dynamic_update_slice.10 = f32[32,64,256]{2,1,0:T(8,128)S(1)} dynamic-update-slice(f32[32,64,256]{2,1,0:T(8,128)S(1)} %broadcast.247.clone.1, f32[32,32,128]{2,1,0:T(8,128)S(1)} %copy.71, s32[]{:T(128)} %constant.42.clone.1, s32[]{:T(128)S(6)} %select_n.109, s32[]{:T(128)S(6)} %select_n.110) | dynamic-update-slice | bytes 1048580 | tf_op jit(solution)/shard_map/dynamic_update_slice | solution.py:150
  263.1 13.9 %dynamic_update_slice.9 = f32[32,64,256]{2,1,0:T(8,128)} dynamic-update-slice(f32[32,64,256]{2,1,0:T(8,128)} %broadcast.247.clone, f32[32,32,128]{2,1,0:T(8,128)S(1)} %copy-done.7, s32[]{:T(128)} %constant.42.clone.1, s32[]{:T(128)S(6)} %select_n.109, s32[]{:T(128)S(6)} %select_n.110) | dynamic-update-slice | bytes 1048580 | tf_op jit(solution)/shard_map/dynamic_update_slice | solution.py:150
  277.1 155.1 %all-reduce.6.cloned.1.call-done = (f32[2,16,64,256]{3,2,1,0:T(8,128)}, f32[2,16,64,256]{3,2,1,0:T(8,128)}) async-done(((f32[2,16,64,256]{3,2,1,0:T(8,128)}, f32[2,16,64,256]{3,2,1,0:T(8,128)}), (f32[2,16,64,256]{3,2,1,0:T(8,128)}, f32[2,16,64,256]{3,2,1,0:T(8,128)})) %all-reduce.6.cloned.1.call-update) | async-done | bytes 4194320 | tf_op jit(solution)/shard_map/psum | solution.py:154
  437.9 6.7 collective-permute-done.7
  444.6 6.7 collective-permute-done.8
  451.3 6.7 collective-permute-done.9
  458.0 6.7 collective-permute-done.10
  466.1 5.3 collective-permute-done.11
  472.8 5.2 collective-permute-done.12
  479.7 5.2 collective-permute-done.13
  510.8 51.6 %all_to_all.15 = f32[8,32,32,128]{3,1,2,0:T(8,128)S(1)} all-to-all(f32[8,32,32,128]{3,1,2,0:T(8,128)S(1)} %copy.78), channel_id=1, replica_groups=mesh['view'=4,'brick'=8] {'brick'}, dimensions={0} | all-to-all | bytes 8388608 | tf_op jit(solution)/shard_map/all_to_all | solution.py:146
  566.5 14.1 %dynamic_update_slice.11 = f32[32,64,256]{2,1,0:T(8,128)} dynamic-update-slice(f32[32,64,256]{2,1,0:T(8,128)} %broadcast.247, f32[32,32,128]{2,1,0:T(8,128)S(1)} %copy.80, s32[]{:T(128)} %constant.42.clone.1, s32[]{:T(128)S(6)} %select_n.109, s32[]{:T(128)S(6)} %select_n.110) | dynamic-update-slice | bytes 1048580 | tf_op jit(solution)/shard_map/dynamic_update_slice | solution.py:150
  580.6 83.5 %all-reduce.4.cloned.1.call-done = f32[2,16,64,256]{3,2,1,0:T(8,128)} async-done(((f32[2,16,64,256]{3,2,1,0:T(8,128)}), f32[2,16,64,256]{3,2,1,0:T(8,128)}) %all-reduce.4.cloned.1.call-update) | async-done | bytes 2097168 | tf_op jit(solution)/shard_map/psum | solution.py:154
  (166 shorter events, 131.3 us)
Async XLA Ops:
  6.5 11.6 %copy-start = (s32[1,1,32]{2,1,0:T(1,128)S(1)}, s32[1,1,32]{2,1,0:T(1,128)}, u32[]{:S(2)}) copy-start(s32[1,1,32]{2,1,0:T(1,128)} %param.20) | copy-start | bytes 388
  13.9 14.3 %collective-permute-start = (bf16[32,32,128]{2,1,0:T(8,128)(2,1)S(1)}, bf16[32,32,128]{2,1,0:T(8,128)(2,1)S(1)}, u32[]{:S(2)}, u32[]{:S(2)}) collective-permute-start(bf16[32,32,128]{2,1,0:T(8,128)(2,1)S(1)} %get-tuple-element.19), channel_id=1, source_target_pairs={{0,1},{1,2},{2,3},{3,4},{4,5},{5,6},{6,7},{7,0},{8,9},{9,10},{10,1... | collective-permute-start | bytes 786440 | tf_op jit(solution)/shard_map/ppermute | solution.py:22
  27.3 9.2 %copy-start.1 = (s32[1,1,32,1]{2,3,1,0:T(1,128)S(1)}, s32[1,1,32,1]{2,3,1,0:T(1,128)}, u32[]{:S(2)}) copy-start(s32[1,1,32,1]{2,3,1,0:T(1,128)} %param.17) | copy-start | bytes 388
  27.3 10.4 %copy-start.2 = (s32[1,1,32]{2,1,0:T(1,128)S(1)}, s32[1,1,32]{2,1,0:T(1,128)}, u32[]{:S(2)}) copy-start(s32[1,1,32]{2,1,0:T(1,128)} %param.18) | copy-start | bytes 388
  27.3 11.7 %copy-start.3 = (s32[1,1,32]{2,1,0:T(1,128)S(1)}, s32[1,1,32]{2,1,0:T(1,128)}, u32[]{:S(2)}) copy-start(s32[1,1,32]{2,1,0:T(1,128)} %param.19) | copy-start | bytes 388
  28.3 7.0 %collective-permute-start.1 = (bf16[32,32,128]{2,1,0:T(8,128)(2,1)S(1)}, bf16[32,32,128]{2,1,0:T(8,128)(2,1)S(1)}, u32[]{:S(2)}, u32[]{:S(2)}) collective-permute-start(bf16[32,32,128]{2,1,0:T(8,128)(2,1)S(1)} %collective-permute-done), channel_id=1, source_target_pairs={{0,1},{1,2},{2,3},{3,4},{4,5},{5,6},{6,7},{7,0},{8,9},{9,10},{10,1... | collective-permute-start | bytes 786440 | tf_op jit(solution)/shard_map/ppermute | solution.py:22
  35.2 6.7 collective-permute-start.2
  41.9 6.7 collective-permute-start.3
  48.6 6.7 collective-permute-start.4
  55.3 6.7 collective-permute-start.5
  62.0 6.9 %collective-permute-start.6 = (bf16[32,32,128]{2,1,0:T(8,128)(2,1)S(1)}, bf16[32,32,128]{2,1,0:T(8,128)(2,1)S(1)}, u32[]{:S(2)}, u32[]{:S(2)}) collective-permute-start(bf16[32,32,128]{2,1,0:T(8,128)(2,1)S(1)} %collective-permute-done.5), channel_id=1, source_target_pairs={{0,1},{1,2},{2,3},{3,4},{4,5},{5,6},{6,7},{7,0},{8,9},{9,10},{10,1... | collective-permute-start | bytes 786440 | tf_op jit(solution)/shard_map/ppermute | solution.py:22
  98.9 53.6 %all-to-all-start.1 = ((f32[8,32,32,128]{3,1,2,0:T(8,128)}), f32[8,32,32,128]{3,1,2,0:T(8,128)}, u32[]{:S(2)}, u32[]{:S(2)}) async-start(f32[8,32,32,128]{3,1,2,0:T(8,128)} %copy.69), calls=%async_computation.1 | async-start | bytes 8388608 | tf_op jit(solution)/shard_map/all_to_all | solution.py:146
  152.5 89.8 %all-to-all-start = ((f32[8,32,32,128]{3,1,2,0:T(8,128)}), f32[8,32,32,128]{3,1,2,0:T(8,128)}, u32[]{:S(2)}, u32[]{:S(2)}) async-start(f32[8,32,32,128]{3,1,2,0:T(8,128)} %copy.64), calls=%async_computation | async-start | bytes 8388608 | tf_op jit(solution)/shard_map/all_to_all | solution.py:146
  157.1 275.1 %all-reduce.6.cloned.1.call-start = ((), (), s32[]{:S(2)}) async-start(), calls=%async_computation.4 | async-start | bytes 8388608 | tf_op jit(solution)/shard_map/psum | solution.py:154
  261.5 15.5 %copy-start.6 = (f32[32,64,256]{2,1,0:T(8,128)}, f32[32,64,256]{2,1,0:T(8,128)S(1)}, u32[]{:S(2)}) copy-start(f32[32,64,256]{2,1,0:T(8,128)S(1)} %dynamic_update_slice.10) | copy-start | bytes 6291460
  277.0 387.1 %all-reduce.4.cloned.1.call-start = ((), (), s32[]{:S(2)}) async-start(), calls=%async_computation.3 | async-start | bytes 4194304 | tf_op jit(solution)/shard_map/psum | solution.py:154
  437.9 6.7 collective-permute-start.7
  444.6 6.7 collective-permute-start.8
  451.3 6.7 collective-permute-start.9
  457.9 6.7 collective-permute-start.10
  464.6 6.7 collective-permute-start.11
  471.3 6.7 collective-permute-start.12
  478.0 6.9 %collective-permute-start.13 = (bf16[32,32,128]{2,1,0:T(8,128)(2,1)S(1)}, bf16[32,32,128]{2,1,0:T(8,128)(2,1)S(1)}, u32[]{:S(2)}, u32[]{:S(2)}) collective-permute-start(bf16[32,32,128]{2,1,0:T(8,128)(2,1)S(1)} %collective-permute-done.12), channel_id=1, source_target_pairs={{0,1},{1,2},{2,3},{3,4},{4,5},{5,6},{6,7},{7,0},{8,9},{9,10},{10,1... | collective-permute-start | bytes 786440 | tf_op jit(solution)/shard_map/ppermute | solution.py:22
  566.5 97.6 %copy-start.5 = (f32[2,16,64,256]{3,2,1,0:T(8,128)S(1)}, f32[2,16,64,256]{3,2,1,0:T(8,128)}, u32[]{:S(2)}) copy-start(f32[2,16,64,256]{3,2,1,0:T(8,128)} %copy-done.4) | copy-start | bytes 6291460
  (5 other events, 7.2 us)
Sparse Core Ops, SparseCore 0:
  277.2 154.9 all-reduce.5
  580.8 83.2 all-reduce.3
